TPU v7x, 256 devices: a whole 4x4x8 slice. The times are simulated.
256 devices in a mesh: dp: 64 (over z, y, core), section: 4 (over x).
Axes of the slice: x: 4, y: 4, z: 8, core: 2. Of those that a mesh axis runs over, the one named last changes fastest.
Arguments:
- query_hidden: bfloat16 [32768, 4096], P('dp', 'section'), may hold values from -0.5 to 0.5
- tool_hidden: bfloat16 [32768, 4096], P('dp', 'section'), may hold values from -0.5 to 0.5
- norm_gain: float32 [4096], P('section'), may hold values from 0.5 to 1.5
- positive_tool: int32 [32768], P('dp'), may hold values from 0 to 511
- hard_owner: int32 [32768, 2], P('dp'), may hold values from 0 to 63, as said below
- hard_row: int32 [32768, 2], P('dp'), may hold values from 0 to 511
- hard_valid: int32 [32768, 2], P('dp'), may hold values from 0 to 1
Outputs:
- query_grad: bfloat16 [32768, 4096], P('dp', 'section')
- tool_grad: bfloat16 [32768, 4096], P('dp', 'section')
- gain_grad: float32 [4096], P('section')
Inputs may be any that keep to these rules, and one draw needn't show every extreme that they name: `hard_owner`: each dp index's valid slots name any one owner at most 32 times; two owners, the same for every dp index and drawn from the seed, are named exactly 32 times by the valid slots of every dp index.
All inputs are finite; a program needn't handle non-finite values.
Results may differ from a plain program's by a relative error of at most 0.0067.
Values may be sent and summed in bfloat16 or wider, within the bound.
A program may use at most 128 MiB of HBM per device.

v0:
```python
import jax
import jax.numpy as jnp
import numpy as np
from jax import lax
from jax.sharding import Mesh
from jax.sharding import PartitionSpec as P

EPSILON = 1e-06
SOFTMAX_TEMP = 0.05
DP = ("dz", "dy", "dc")


def softmax_grads(shard_scores, negative_scores, positive, valid_mask):
    selected_rows = lax.broadcasted_iota(jnp.int32, shard_scores.shape, 1) == positive[:, None]
    softmax_weights = jnp.exp(shard_scores / SOFTMAX_TEMP)
    shard_probabilities = softmax_weights / jnp.sum(softmax_weights, axis=1, keepdims=True)
    positive_score = jnp.sum(jnp.where(selected_rows, shard_scores, 0.0), axis=1)
    positive_weight = jnp.exp(positive_score / SOFTMAX_TEMP)
    negative_weights = jnp.where(valid_mask > 0, jnp.exp(negative_scores / SOFTMAX_TEMP), 0.0)
    negative_weight_sum = positive_weight + jnp.sum(negative_weights, axis=1)
    shard_gradients = (
        (
            shard_probabilities
            + jnp.where(selected_rows, (positive_weight / negative_weight_sum - 2.0)[:, None], 0.0)
        )
        / SOFTMAX_TEMP
    ).astype(jnp.bfloat16)
    negative_gradients = (negative_weights / (negative_weight_sum[:, None] * SOFTMAX_TEMP)).astype(
        jnp.bfloat16
    )
    return (shard_gradients, negative_gradients)


def body(query_hidden, tool_hidden, norm_gain, positive_tool, hard_owner, hard_row, hard_valid):
    query_count, features = query_hidden.shape
    tool_count = tool_hidden.shape[0]
    per_query = hard_owner.shape[1]
    slots = query_count * per_query
    group_size = lax.axis_size(DP)
    capacity = max(2, 2 * query_count * per_query // group_size)
    places = group_size * capacity
    owners = hard_owner.reshape(-1)
    wanted_rows = hard_row.reshape(-1)
    usable = hard_valid.reshape(-1) > 0
    slot_ids = jnp.arange(slots, dtype=jnp.int32)
    same_earlier = (
        (owners[:, None] == owners[None, :])
        & usable[None, :]
        & (slot_ids[None, :] < slot_ids[:, None])
    )
    slot_place = jnp.sum(same_earlier.astype(jnp.int32), axis=1)
    target = jnp.where(usable, owners * capacity + slot_place, places)
    place_ids = jnp.arange(places, dtype=jnp.int32)
    slot_at = target[:, None] == place_ids[None, :]
    requests = jnp.sum(jnp.where(slot_at, wanted_rows[:, None], 0), axis=0).reshape(
        group_size, capacity
    )
    indices = lax.all_to_all(requests, DP, 0, 0, tiled=True).reshape(-1)
    query_scaled = query_hidden.astype(jnp.float32) * norm_gain
    tool_scaled = tool_hidden.astype(jnp.float32) * norm_gain
    query_squares, tool_squares = lax.psum(
        (jnp.sum(query_scaled * query_scaled, axis=1), jnp.sum(tool_scaled * tool_scaled, axis=1)),
        "section",
    )
    query_norm = jnp.sqrt(query_squares + EPSILON)
    tool_norm = jnp.sqrt(tool_squares + EPSILON)
    query_unit32 = query_scaled / query_norm[:, None]
    tool_unit32 = tool_scaled / tool_norm[:, None]
    query_unit = query_unit32.astype(jnp.bfloat16)
    tool_unit = tool_unit32.astype(jnp.bfloat16)
    pick_tool = (indices[:, None] == jnp.arange(tool_count, dtype=jnp.int32)[None, :]).astype(
        jnp.bfloat16
    )
    answers = jnp.dot(pick_tool, tool_unit, preferred_element_type=jnp.float32).astype(jnp.bfloat16)
    slot_of_query = slot_at.reshape(query_count, per_query, places).any(axis=1)
    pick_query = slot_of_query.T.astype(jnp.bfloat16)
    sent_queries = jnp.dot(pick_query, query_unit, preferred_element_type=jnp.float32).astype(
        jnp.bfloat16
    )
    payload = jnp.concatenate(
        [
            answers.reshape(group_size, capacity, features),
            sent_queries.reshape(group_size, capacity, features),
        ],
        axis=1,
    )
    received = lax.all_to_all(payload, DP, 0, 0, tiled=True)
    back = received[:, :capacity].reshape(places, features)
    arrived = received[:, capacity:].reshape(places, features)
    local_part = lax.dot_general(
        query_unit, tool_unit, (((1,), (1,)), ((), ())), preferred_element_type=jnp.float32
    )
    hard_units = jnp.dot(
        slot_at.astype(jnp.bfloat16), back, preferred_element_type=jnp.float32
    ).reshape(query_count, per_query, features)
    hard_part = jnp.einsum(
        "qd,qkd->qk", query_unit.astype(jnp.float32), hard_units, preferred_element_type=jnp.float32
    )
    shard_scores, negative_scores = (
        lax.psum(local_part.astype(jnp.bfloat16), "section").astype(jnp.float32),
        lax.psum(hard_part.astype(jnp.bfloat16), "section").astype(jnp.float32),
    )
    shard_gradients, negative_gradients = softmax_grads(
        shard_scores, negative_scores, positive_tool, hard_valid
    )
    query_pull = jnp.dot(shard_gradients, tool_unit, preferred_element_type=jnp.float32)
    query_pull = query_pull + jnp.einsum(
        "qk,qkd->qd",
        negative_gradients.astype(jnp.float32),
        hard_units,
        preferred_element_type=jnp.float32,
    )
    sent_grads = jnp.sum(
        jnp.where(slot_at, negative_gradients.reshape(-1)[:, None].astype(jnp.float32), 0.0), axis=0
    ).astype(jnp.bfloat16)
    arrived_grads = lax.all_to_all(
        sent_grads.reshape(group_size, capacity), DP, 0, 0, tiled=True
    ).reshape(-1)
    weights = jnp.where(
        jnp.arange(tool_count, dtype=jnp.int32)[:, None] == indices[None, :],
        arrived_grads[None, :],
        0.0,
    ).astype(jnp.bfloat16)
    tool_pull = lax.dot_general(
        shard_gradients, query_unit, (((0,), (0,)), ((), ())), preferred_element_type=jnp.float32
    )
    tool_pull = tool_pull + jnp.dot(weights, arrived, preferred_element_type=jnp.float32)
    query_inner, tool_inner = lax.psum(
        (jnp.sum(query_unit32 * query_pull, axis=1), jnp.sum(tool_unit32 * tool_pull, axis=1)),
        "section",
    )
    query_back = (query_pull - query_unit32 * query_inner[:, None]) / query_norm[:, None]
    tool_back = (tool_pull - tool_unit32 * tool_inner[:, None]) / tool_norm[:, None]
    query_grad = (query_back * norm_gain).astype(jnp.bfloat16)
    tool_grad = (tool_back * norm_gain).astype(jnp.bfloat16)
    gain_terms = jnp.sum(query_back * query_hidden.astype(jnp.float32), axis=0) + jnp.sum(
        tool_back * tool_hidden.astype(jnp.float32), axis=0
    )
    gain_grad = lax.psum(lax.psum(lax.psum(gain_terms, "dc"), "dy"), "dz")
    return (query_grad, tool_grad, gain_grad)


def split_dp(mesh):
    dp = mesh.shape["dp"]
    cores = 2 if dp % 2 == 0 else 1
    rest = dp // cores
    ys = 4 if rest % 4 == 0 else 1
    devices = np.asarray(mesh.devices).reshape(rest // ys, ys, cores, mesh.shape["section"])
    return Mesh(devices, DP + ("section",))


def solution(mesh):
    fine = split_dp(mesh)
    return jax.shard_map(
        body,
        mesh=fine,
        in_specs=(
            P(DP, "section"),
            P(DP, "section"),
            P("section"),
            P(DP),
            P(DP, None),
            P(DP, None),
            P(DP, None),
        ),
        out_specs=(P(DP, "section"), P(DP, "section"), P("section")),
        check_vma=False,
    )
```

profile of v0, /device:TPU:2, one launch (start us, length us, event | category | flops | bytes accessed | tf_op | source)
XLA Modules:
  0.0 356.6 jit_solution(10480050438670012715)
XLA Ops:
  12.8 12.1 %all-to-all-start = ((s32[64,1,32]{2,1,0:T(1,128)}), s32[64,1,32]{2,1,0:T(1,128)S(1)}, u32[]{:S(2)}, u32[]{:S(2)}) async-start(s32[64,1,32]{2,1,0:T(1,128)} %bitcast.2), calls=%async_computation | async-start | bytes 65536 | tf_op jit(solution)/shard_map/all_to_all | solution.py:58
  27.0 8.6 %all-reduce.1 = (f32[512]{0:T(512)S(1)}, f32[512]{0:T(512)S(1)}) all-reduce(f32[512]{0:T(512)S(1)} %get-tuple-element.8, f32[512]{0:T(512)S(1)} %get-tuple-element.7), channel_id=1, replica_groups=mesh['dz'=8,'dy'=4,'dc'=2,'section'=4] {'section'}, use_global_device_ids=true, to_apply=%region_1.2 | all-reduce | flops 1024 | bytes 8192 | tf_op jit(solution)/shard_map/psum | solution.py:61
  36.9 4.5 %convolution_convert_fusion = bf16[2048,1024]{1,0:T(8,128)(2,1)} fusion(pred[512,2048]{1,0:T(8,128)(4,1)S(1)} %fusion.3, f32[512]{0:T(512)S(1)} %add_sqrt_fusion.1, f32[1024]{0:T(1024)S(1)} %copy-done.5, bf16[512,1024]{1,0:T(8,128)(2,1)S(1)} %copy-done), kind=kOutput, calls=%fused_computation.18 | convolution fusion | flops 2151677952 | bytes 6297600 | tf_op jit(solution)/shard_map/dot_general | solution.py:77
  42.7 4.2 %fusion.8 = bf16[2048,1024]{1,0:T(8,128)(2,1)} fusion(s32[2048]{0:T(1024)S(1)} %eq.106, bf16[512,1024]{1,0:T(8,128)(2,1)S(1)} %copy-done.1, f32[512]{0:T(512)S(1)} %add_sqrt_fusion, f32[1024]{0:T(1024)S(1)} %copy-done.5), kind=kOutput, calls=%fused_computation.17 | convolution fusion | flops 2152726528 | bytes 5257216 | tf_op jit(solution)/shard_map/dot_general | solution.py:74
  46.9 8.5 %pad_maximum_fusion = bf16[64,64,1024]{2,1,0:T(8,128)(2,1)} fusion(bf16[64,32,1024]{2,1,0:T(8,128)(2,1)} %bitcast.23, bf16[64,32,1024]{2,1,0:T(8,128)(2,1)} %bitcast.25), kind=kLoop, calls=%fused_computation | loop fusion | flops 16777216 | bytes 16777216 | tf_op jit(solution)/shard_map/concatenate | solution.py:80
  55.4 10.6 %all-to-all-start.1 = ((bf16[64,64,1024]{2,1,0:T(8,128)(2,1)}), bf16[64,64,1024]{2,1,0:T(8,128)(2,1)}, u32[]{:S(2)}, u32[]{:S(2)}) async-start(bf16[64,64,1024]{2,1,0:T(8,128)(2,1)} %pad_maximum_fusion), calls=%async_computation.1 | async-start | bytes 16777216 | tf_op jit(solution)/shard_map/all_to_all | solution.py:87
  68.2 49.4 %all-reduce.4.cloned.1.call-done = bf16[512,512]{1,0:T(8,128)(2,1)} async-done(((bf16[512,512]{1,0:T(8,128)(2,1)}), bf16[512,512]{1,0:T(8,128)(2,1)}) %all-reduce.4.cloned.1.call-update) | async-done | bytes 524304 | tf_op jit(solution)/shard_map/psum | solution.py:100
  119.1 133.1 %all-to-all-done.1 = bf16[64,64,1024]{2,1,0:T(8,128)(2,1)} async-done(((bf16[64,64,1024]{2,1,0:T(8,128)(2,1)}), bf16[64,64,1024]{2,1,0:T(8,128)(2,1)}, u32[]{:S(2)}, u32[]{:S(2)}) %all-to-all-start.1) | async-done | bytes 8388640 | tf_op jit(solution)/shard_map/all_to_all | solution.py:87
  252.2 5.4 %fusion.50 = (bf16[64,32,1024]{2,1,0:T(8,128)(2,1)}, bf16[64,32,1024]{2,1,0:T(8,128)(2,1)S(1)}) fusion(bf16[64,64,1024]{2,1,0:T(8,128)(2,1)} %all-to-all-done.1), kind=kLoop, calls=%fused_computation.78 | loop fusion | bytes 16777216 | tf_op jit(solution)/shard_map/slice | solution.py:89
  257.5 4.8 %fusion.1 = bf16[512,2,1024]{2,0,1:T(8,128)(2,1)S(1)} fusion(bf16[2048,1024,1]{1,0,2:T(8,128)(2,1)S(1)} %bitcast.24, s32[512,2]{0,1:T(2,128)S(1)} %add_select_fusion.1), kind=kOutput, calls=%fused_computation.7 | convolution fusion | flops 4297064448 | bytes 6295552 | tf_op jit(solution)/shard_map/dot_general | solution.py:93
  263.7 8.8 %fusion.11 = bf16[512,1,2]{2,1,0:T(2,128)(2,1)S(1)} fusion(bf16[512,2,1024]{2,0,1:T(8,128)(2,1)S(1)} %fusion.1, bf16[512,1024,1]{1,0,2:T(8,128)(2,1)S(1)} %fusion.47), kind=kOutput, calls=%fused_computation.21 | convolution fusion | flops 2097152 | bytes 3147776 | tf_op jit(solution)/shard_map/qd,qkd->qk/dot_general | solution.py:96
  272.7 10.1 %psum.66 = bf16[512,2]{0,1:T(2,128)(2,1)S(1)} all-reduce(bf16[512,2]{0,1:T(2,128)(2,1)S(1)} %bitcast.27), channel_id=1, replica_groups=mesh['dz'=8,'dy'=4,'dc'=2,'section'=4] {'section'}, use_global_device_ids=true, to_apply=%region_10.11 | all-reduce | flops 1024 | bytes 4096 | tf_op jit(solution)/shard_map/psum | solution.py:101
  285.1 6.4 %all-to-all-start.2 = ((bf16[64,1,32]{2,1,0:T(2,128)(2,1)}), bf16[64,1,32]{2,1,0:T(2,128)(2,1)S(1)}, u32[]{:S(2)}, u32[]{:S(2)}) async-start(bf16[64,1,32]{2,1,0:T(2,128)(2,1)} %convert_element_type.99), calls=%async_computation.2 | async-start | bytes 65536 | tf_op jit(solution)/shard_map/all_to_all | solution.py:116
  291.8 4.1 %fusion.9 = f32[512,1,1024]{2,1,0:T(1,128)S(1)} fusion(bf16[512,2,1]{1,2,0:T(2,128)(2,1)S(1)} %copy.44, bf16[512,2,1024]{2,0,1:T(8,128)(2,1)} %copy-done.9), kind=kOutput, calls=%fused_computation.19 | convolution fusion | flops 2097152 | bytes 4196352 | tf_op jit(solution)/shard_map/qk,qkd->qd/dot_general | solution.py:107
  295.9 2.5 bitcast_add_fusion
  298.4 2.5 all-to-all-done.2
  301.1 4.7 %fusion.21 = f32[512,1024]{1,0:T(8,128)S(1)} fusion(bf16[2048,1024]{1,0:T(8,128)(2,1)} %bitcast.22, s32[2048]{0:T(1024)S(1)} %eq.106, bf16[2048]{0:T(1024)(128)(2,1)S(1)} %broadcast_in_dim.95), kind=kOutput, calls=%fused_computation.35 | convolution fusion | flops 2149580800 | bytes 6303744 | tf_op jit(solution)/shard_map/dot_general | solution.py:127
  305.7 2.9 multiply_reduce_fusion
  308.7 7.7 %all-reduce = (f32[512]{0:T(512)S(1)}, f32[512]{0:T(512)S(1)}) all-reduce(f32[512]{0:T(512)S(1)} %get-tuple-element.6, f32[512]{0:T(512)S(1)} %get-tuple-element.5), channel_id=1, replica_groups=mesh['dz'=8,'dy'=4,'dc'=2,'section'=4] {'section'}, use_global_device_ids=true, to_apply=%region_13.14 | all-reduce | flops 1024 | bytes 8192 | tf_op jit(solution)/shard_map/psum | solution.py:128
  316.4 2.4 fusion.20
  318.8 1.9 fusion.19
  320.6 2.4 psum.69
  323.1 8.8 %psum.70 = f32[1024]{0:T(1024)S(1)} all-reduce(f32[1024]{0:T(1024)S(1)} %psum.69), channel_id=1, replica_groups=mesh['dz'=8,'dy'=4,'dc'=2,'section'=4] {'dy'}, use_global_device_ids=true, to_apply=%region_20.21 | all-reduce | flops 1024 | bytes 8192 | tf_op jit(solution)/shard_map/psum | solution.py:139
  331.8 16.7 %psum.71 = f32[1024]{0:T(1024)} all-reduce(f32[1024]{0:T(1024)S(1)} %psum.70), channel_id=1, replica_groups=mesh['dz'=8,'dy'=4,'dc'=2,'section'=4] {'dz'}, use_global_device_ids=true, to_apply=%region_21.22 | all-reduce | flops 1024 | bytes 8192 | tf_op jit(solution)/shard_map/psum | solution.py:139
  (60 shorter events, 19.3 us)
Async XLA Ops:
  7.2 28.6 %copy-start.7 = (s32[512,2]{0,1:T(2,128)S(1)}, s32[512,2]{0,1:T(2,128)}, u32[]{:S(2)}) copy-start(s32[512,2]{0,1:T(2,128)} %param.11) | copy-start | bytes 12292
  7.2 28.6 %copy-start.6 = (s32[512,2]{0,1:T(2,128)S(1)}, s32[512,2]{0,1:T(2,128)}, u32[]{:S(2)}) copy-start(s32[512,2]{0,1:T(2,128)} %param.13) | copy-start | bytes 12292
  7.2 18.0 %copy-start = (bf16[512,1024]{1,0:T(8,128)(2,1)S(1)}, bf16[512,1024]{1,0:T(8,128)(2,1)}, u32[]{:S(2)}) copy-start(bf16[512,1024]{1,0:T(8,128)(2,1)} %param.7) | copy-start | bytes 3145732
  10.8 26.1 %copy-start.5 = (f32[1024]{0:T(1024)S(1)}, f32[1024]{0:T(1024)}, u32[]{:S(2)}) copy-start(f32[1024]{0:T(1024)} %param.9) | copy-start | bytes 12292
  12.8 28.6 %all-to-all-start = ((s32[64,1,32]{2,1,0:T(1,128)}), s32[64,1,32]{2,1,0:T(1,128)S(1)}, u32[]{:S(2)}, u32[]{:S(2)}) async-start(s32[64,1,32]{2,1,0:T(1,128)} %bitcast.2), calls=%async_computation | async-start | bytes 65536 | tf_op jit(solution)/shard_map/all_to_all | solution.py:58
  36.9 5.8 %copy-start.1 = (bf16[512,1024]{1,0:T(8,128)(2,1)S(1)}, bf16[512,1024]{1,0:T(8,128)(2,1)}, u32[]{:S(2)}) copy-start(bf16[512,1024]{1,0:T(8,128)(2,1)} %param.8) | copy-start | bytes 3145732
  55.4 196.7 %all-to-all-start.1 = ((bf16[64,64,1024]{2,1,0:T(8,128)(2,1)}), bf16[64,64,1024]{2,1,0:T(8,128)(2,1)}, u32[]{:S(2)}, u32[]{:S(2)}) async-start(bf16[64,64,1024]{2,1,0:T(8,128)(2,1)} %pad_maximum_fusion), calls=%async_computation.1 | async-start | bytes 16777216 | tf_op jit(solution)/shard_map/all_to_all | solution.py:87
  66.0 51.6 %all-reduce.4.cloned.1.call-start = ((), (), s32[]{:S(2)}) async-start(), calls=%async_computation.3 | async-start | bytes 1048576 | tf_op jit(solution)/shard_map/psum | solution.py:100
  67.9 49.7 %copy-start.8 = (s32[512]{0:T(512)S(1)}, s32[512]{0:T(512)}, u32[]{:S(2)}) copy-start(s32[512]{0:T(512)} %param.10) | copy-start | bytes 6148
  262.4 1.3 copy-start.9
  285.1 15.7 %all-to-all-start.2 = ((bf16[64,1,32]{2,1,0:T(2,128)(2,1)}), bf16[64,1,32]{2,1,0:T(2,128)(2,1)S(1)}, u32[]{:S(2)}, u32[]{:S(2)}) async-start(bf16[64,1,32]{2,1,0:T(2,128)(2,1)} %convert_element_type.99), calls=%async_computation.2 | async-start | bytes 65536 | tf_op jit(solution)/shard_map/all_to_all | solution.py:116
  291.7 4.1 %copy-start.4 = (bf16[512,512]{1,0:T(8,128)(2,1)S(1)}, bf16[512,512]{1,0:T(8,128)(2,1)}, u32[]{:S(2)}) copy-start(bf16[512,512]{1,0:T(8,128)(2,1)} %all-reduce.4.cloned.1.call-done) | copy-start | bytes 1572868
  301.1 4.7 %copy-start.2 = (f32[512,1024]{1,0:T(8,128)S(1)}, f32[512,1024]{1,0:T(8,128)}, u32[]{:S(2)}) copy-start(f32[512,1024]{1,0:T(8,128)} %bitcast_add_fusion) | copy-start | bytes 6291460
  316.4 2.4 copy-start.3
Sparse Core Ops, SparseCore 0:
  69.7 47.8 all-reduce.3
where the time goes:
time: 357 us
  waiting for transfers between devices  185 us (52%)
  blocking collectives  54.3 us (15%)
  matrix products  38.2 us (11%)
  starting transfers between devices  29.3 us (8%)
  other arithmetic  23.3 us (7%)
  between operations  14.3 us (4%)
  local copies, waits for them, and re-layouts  12.2 us (3%)
    all_to_all x1, waiting for transfers between devices, body(): received = lax.all_to_all(payload, DP, 0, 0, tiled=True)  133 us
    psum x1, waiting for transfers between devices, body(): lax.psum(local_part.astype(jnp.bfloat16), 'section').astype(jnp.float32)  49.4 us
    psum x3, blocking collectives, body(): gain_grad = lax.psum(lax.psum(lax.psum(gain_terms, 'dc'), 'dy'), 'dz')  27.9 us
    all_to_all x1, starting transfers between devices, body(): indices = lax.all_to_all(requests, DP, 0, 0, tiled=True).reshape(-1)  12.1 us
    all_to_all x1, starting transfers between devices, body(): received = lax.all_to_all(payload, DP, 0, 0, tiled=True)  10.6 us
    psum x1, blocking collectives, body(): lax.psum(hard_part.astype(jnp.bfloat16), 'section').astype(jnp.float32)  10.1 us
    dot_general x1, matrix products, body(): jnp.einsum('qd,qkd->qk', query_unit.astype(jnp.float32), hard_units, pref...  8.83 us
    psum x1, blocking collectives, body(): lax.psum((jnp.sum(query_scaled * query_scaled, axis=1), jnp.sum(tool_scal...  8.62 us
  transfers between devices with their start and end apart: 4, of which 3 were waited for; matrix products, arithmetic and copies ran while one was open for 5% of the time, Pallas kernels for 0%

commit v1 on v0

--- a/solution.py
+++ b/solution.py
@@ -1,3 +1,4 @@
+import functools
 import jax
 import jax.numpy as jnp
 import numpy as np
@@ -8,6 +9,14 @@
 EPSILON = 1e-06
 SOFTMAX_TEMP = 0.05
 DP = ("dz", "dy", "dc")
+
+
+def turn_sites(vector, comm_axis):
+    r2 = jnp.sum(lax.all_gather(vector, comm_axis), 0)
+    return r2
+
+
+rails_clear = functools.partial(turn_sites, comm_axis="section")
 
 
 def softmax_grads(shard_scores, negative_scores, positive, valid_mask):
@@ -98,7 +107,7 @@
     )
     shard_scores, negative_scores = (
         lax.psum(local_part.astype(jnp.bfloat16), "section").astype(jnp.float32),
-        lax.psum(hard_part.astype(jnp.bfloat16), "section").astype(jnp.float32),
+        rails_clear(hard_part.astype(jnp.bfloat16)).astype(jnp.float32),
     )
     shard_gradients, negative_gradients = softmax_grads(
         shard_scores, negative_scores, positive_tool, hard_valid

time: 357 us -> 360 us (level)
    all_gather x0 -> x1, blocking collectives: none -> 10.9 us  [turn_sites(): r2 = jnp.sum(lax.all_gather(vector, comm_axis), 0)]
    psum x1 -> x0, blocking collectives: 10.1 us -> none  [body(): lax.psum(hard_part.astype(jnp.bfloat16), 'section').astype(jnp.float32)]
where the time goes in v1:
time: 360 us; the launch traced here: 359 us
  waiting for transfers between devices  185 us (51%)
  blocking collectives  57.1 us (16%)
  matrix products  38.2 us (11%)
  starting transfers between devices  29.2 us (8%)
  other arithmetic  23.3 us (6%)
  between operations  14.3 us (4%)
  local copies, waits for them, and re-layouts  12.2 us (3%)
    all_to_all x1, waiting for transfers between devices, body(): received = lax.all_to_all(payload, DP, 0, 0, tiled=True)  133 us
    psum x1, waiting for transfers between devices, body(): lax.psum(local_part.astype(jnp.bfloat16), 'section').astype(jnp.float32)  49.4 us
    psum x3, blocking collectives, body(): gain_grad = lax.psum(lax.psum(lax.psum(gain_terms, 'dc'), 'dy'), 'dz')  27.9 us
    all_to_all x1, starting transfers between devices, body(): indices = lax.all_to_all(requests, DP, 0, 0, tiled=True).reshape(-1)  12.1 us
    all_gather x1, blocking collectives, turn_sites(): r2 = jnp.sum(lax.all_gather(vector, comm_axis), 0)  10.9 us
    all_to_all x1, starting transfers between devices, body(): received = lax.all_to_all(payload, DP, 0, 0, tiled=True)  10.6 us
    psum x1, blocking collectives, body(): lax.psum((jnp.sum(query_unit32 * query_pull, axis=1), jnp.sum(tool_unit32...  9.65 us
    dot_general x1, matrix products, body(): jnp.einsum('qd,qkd->qk', query_unit.astype(jnp.float32), hard_units, pref...  8.83 us
  transfers between devices with their start and end apart: 4, of which 3 were waited for; matrix products, arithmetic and copies ran while one was open for 5% of the time, Pallas kernels for 0%

profile of v1, /device:TPU:2, one launch (start us, length us, event | category | flops | bytes accessed | tf_op | source)
XLA Modules:
  0.0 359.4 jit_solution(1573743411470300359)
XLA Ops:
  12.8 12.1 %all-to-all-start = ((s32[64,1,32]{2,1,0:T(1,128)}), s32[64,1,32]{2,1,0:T(1,128)S(1)}, u32[]{:S(2)}, u32[]{:S(2)}) async-start(s32[64,1,32]{2,1,0:T(1,128)} %bitcast.2), calls=%async_computation | async-start | bytes 65536 | tf_op jit(solution)/shard_map/all_to_all | solution.py:67
  27.0 8.6 %all-reduce.1 = (f32[512]{0:T(512)S(1)}, f32[512]{0:T(512)S(1)}) all-reduce(f32[512]{0:T(512)S(1)} %get-tuple-element.8, f32[512]{0:T(512)S(1)} %get-tuple-element.7), channel_id=1, replica_groups=mesh['dz'=8,'dy'=4,'dc'=2,'section'=4] {'section'}, use_global_device_ids=true, to_apply=%region_1.2 | all-reduce | flops 1024 | bytes 8192 | tf_op jit(solution)/shard_map/psum | solution.py:70
  36.9 4.5 %convolution_convert_fusion = bf16[2048,1024]{1,0:T(8,128)(2,1)} fusion(pred[512,2048]{1,0:T(8,128)(4,1)S(1)} %fusion.3, f32[512]{0:T(512)S(1)} %add_sqrt_fusion.1, f32[1024]{0:T(1024)S(1)} %copy-done.5, bf16[512,1024]{1,0:T(8,128)(2,1)S(1)} %copy-done), kind=kOutput, calls=%fused_computation.18 | convolution fusion | flops 2151677952 | bytes 6297600 | tf_op jit(solution)/shard_map/dot_general | solution.py:86
  42.7 4.2 %fusion.8 = bf16[2048,1024]{1,0:T(8,128)(2,1)} fusion(s32[2048]{0:T(1024)S(1)} %eq.106, bf16[512,1024]{1,0:T(8,128)(2,1)S(1)} %copy-done.1, f32[512]{0:T(512)S(1)} %add_sqrt_fusion, f32[1024]{0:T(1024)S(1)} %copy-done.5), kind=kOutput, calls=%fused_computation.17 | convolution fusion | flops 2152726528 | bytes 5257216 | tf_op jit(solution)/shard_map/dot_general | solution.py:83
  46.9 8.5 %pad_maximum_fusion = bf16[64,64,1024]{2,1,0:T(8,128)(2,1)} fusion(bf16[64,32,1024]{2,1,0:T(8,128)(2,1)} %bitcast.25, bf16[64,32,1024]{2,1,0:T(8,128)(2,1)} %bitcast.27), kind=kLoop, calls=%fused_computation | loop fusion | flops 16777216 | bytes 16777216 | tf_op jit(solution)/shard_map/concatenate | solution.py:89
  55.4 10.6 %all-to-all-start.1 = ((bf16[64,64,1024]{2,1,0:T(8,128)(2,1)}), bf16[64,64,1024]{2,1,0:T(8,128)(2,1)}, u32[]{:S(2)}, u32[]{:S(2)}) async-start(bf16[64,64,1024]{2,1,0:T(8,128)(2,1)} %pad_maximum_fusion), calls=%async_computation.1 | async-start | bytes 16777216 | tf_op jit(solution)/shard_map/all_to_all | solution.py:96
  68.2 49.4 %all-reduce.4.cloned.1.call-done = bf16[512,512]{1,0:T(8,128)(2,1)} async-done(((bf16[512,512]{1,0:T(8,128)(2,1)}), bf16[512,512]{1,0:T(8,128)(2,1)}) %all-reduce.4.cloned.1.call-update) | async-done | bytes 524304 | tf_op jit(solution)/shard_map/psum | solution.py:109
  119.1 133.1 %all-to-all-done.1 = bf16[64,64,1024]{2,1,0:T(8,128)(2,1)} async-done(((bf16[64,64,1024]{2,1,0:T(8,128)(2,1)}), bf16[64,64,1024]{2,1,0:T(8,128)(2,1)}, u32[]{:S(2)}, u32[]{:S(2)}) %all-to-all-start.1) | async-done | bytes 8388640 | tf_op jit(solution)/shard_map/all_to_all | solution.py:96
  252.2 5.4 %fusion.50 = (bf16[64,32,1024]{2,1,0:T(8,128)(2,1)}, bf16[64,32,1024]{2,1,0:T(8,128)(2,1)S(1)}) fusion(bf16[64,64,1024]{2,1,0:T(8,128)(2,1)} %all-to-all-done.1), kind=kLoop, calls=%fused_computation.78 | loop fusion | bytes 16777216 | tf_op jit(solution)/shard_map/slice | solution.py:98
  257.5 4.8 %fusion.1 = bf16[512,2,1024]{2,0,1:T(8,128)(2,1)S(1)} fusion(bf16[2048,1024,1]{1,0,2:T(8,128)(2,1)S(1)} %bitcast.26, s32[512,2]{0,1:T(2,128)S(1)} %add_select_fusion.1), kind=kOutput, calls=%fused_computation.7 | convolution fusion | flops 4297064448 | bytes 6295552 | tf_op jit(solution)/shard_map/dot_general | solution.py:102
  263.7 8.8 %fusion.11 = bf16[512,1,2]{2,1,0:T(2,128)(2,1)S(1)} fusion(bf16[512,2,1024]{2,0,1:T(8,128)(2,1)S(1)} %fusion.1, bf16[512,1024,1]{1,0,2:T(8,128)(2,1)S(1)} %fusion.47), kind=kOutput, calls=%fused_computation.21 | convolution fusion | flops 2097152 | bytes 3147776 | tf_op jit(solution)/shard_map/qd,qkd->qk/dot_general | solution.py:105
  272.7 10.9 %all-gather = bf16[2048,2]{0,1:T(2,128)(2,1)S(1)} all-gather(bf16[512,2]{0,1:T(2,128)(2,1)S(1)} %bitcast.29), channel_id=2, replica_groups=mesh['dz'=8,'dy'=4,'dc'=2,'section'=4] {'section'}, dimensions={0}, use_global_device_ids=true | all-gather | bytes 10240 | tf_op jit(solution)/shard_map/all_gather | solution.py:15
  286.0 6.3 %all-to-all-start.2 = ((bf16[64,1,32]{2,1,0:T(2,128)(2,1)}), bf16[64,1,32]{2,1,0:T(2,128)(2,1)S(1)}, u32[]{:S(2)}, u32[]{:S(2)}) async-start(bf16[64,1,32]{2,1,0:T(2,128)(2,1)} %convert_element_type.101), calls=%async_computation.2 | async-start | bytes 65536 | tf_op jit(solution)/shard_map/all_to_all | solution.py:125
  292.5 4.1 %fusion.9 = f32[512,1,1024]{2,1,0:T(1,128)S(1)} fusion(bf16[512,2,1]{1,2,0:T(2,128)(2,1)S(1)} %copy.35, bf16[512,2,1024]{2,0,1:T(8,128)(2,1)} %copy-done.9), kind=kOutput, calls=%fused_computation.19 | convolution fusion | flops 2097152 | bytes 4196352 | tf_op jit(solution)/shard_map/qk,qkd->qd/dot_general | solution.py:116
  296.6 2.5 bitcast_add_fusion
  299.1 2.5 all-to-all-done.2
  301.8 4.7 %fusion.21 = f32[512,1024]{1,0:T(8,128)S(1)} fusion(bf16[2048,1024]{1,0:T(8,128)(2,1)} %bitcast.24, s32[2048]{0:T(1024)S(1)} %eq.106, bf16[2048]{0:T(1024)(128)(2,1)S(1)} %broadcast_in_dim.95), kind=kOutput, calls=%fused_computation.35 | convolution fusion | flops 2149580800 | bytes 6303744 | tf_op jit(solution)/shard_map/dot_general | solution.py:136
  306.5 2.9 multiply_reduce_fusion
  309.5 9.7 %all-reduce = (f32[512]{0:T(512)S(1)}, f32[512]{0:T(512)S(1)}) all-reduce(f32[512]{0:T(512)S(1)} %get-tuple-element.6, f32[512]{0:T(512)S(1)} %get-tuple-element.5), channel_id=1, replica_groups=mesh['dz'=8,'dy'=4,'dc'=2,'section'=4] {'section'}, use_global_device_ids=true, to_apply=%region_13.14 | all-reduce | flops 1024 | bytes 8192 | tf_op jit(solution)/shard_map/psum | solution.py:137
  319.1 2.4 fusion.20
  321.5 1.9 fusion.19
  323.4 2.4 psum.61
  325.8 8.8 %psum.62 = f32[1024]{0:T(1024)S(1)} all-reduce(f32[1024]{0:T(1024)S(1)} %psum.61), channel_id=1, replica_groups=mesh['dz'=8,'dy'=4,'dc'=2,'section'=4] {'dy'}, use_global_device_ids=true, to_apply=%region_20.21 | all-reduce | flops 1024 | bytes 8192 | tf_op jit(solution)/shard_map/psum | solution.py:148
  334.6 16.7 %psum.63 = f32[1024]{0:T(1024)} all-reduce(f32[1024]{0:T(1024)S(1)} %psum.62), channel_id=1, replica_groups=mesh['dz'=8,'dy'=4,'dc'=2,'section'=4] {'dz'}, use_global_device_ids=true, to_apply=%region_21.22 | all-reduce | flops 1024 | bytes 8192 | tf_op jit(solution)/shard_map/psum | solution.py:148
  (62 shorter events, 19.4 us)
Async XLA Ops:
  7.2 28.6 %copy-start.7 = (s32[512,2]{0,1:T(2,128)S(1)}, s32[512,2]{0,1:T(2,128)}, u32[]{:S(2)}) copy-start(s32[512,2]{0,1:T(2,128)} %param.11) | copy-start | bytes 12292
  7.2 28.6 %copy-start.6 = (s32[512,2]{0,1:T(2,128)S(1)}, s32[512,2]{0,1:T(2,128)}, u32[]{:S(2)}) copy-start(s32[512,2]{0,1:T(2,128)} %param.13) | copy-start | bytes 12292
  7.2 18.0 %copy-start = (bf16[512,1024]{1,0:T(8,128)(2,1)S(1)}, bf16[512,1024]{1,0:T(8,128)(2,1)}, u32[]{:S(2)}) copy-start(bf16[512,1024]{1,0:T(8,128)(2,1)} %param.7) | copy-start | bytes 3145732
  10.8 26.1 %copy-start.5 = (f32[1024]{0:T(1024)S(1)}, f32[1024]{0:T(1024)}, u32[]{:S(2)}) copy-start(f32[1024]{0:T(1024)} %param.9) | copy-start | bytes 12292
  12.8 28.6 %all-to-all-start = ((s32[64,1,32]{2,1,0:T(1,128)}), s32[64,1,32]{2,1,0:T(1,128)S(1)}, u32[]{:S(2)}, u32[]{:S(2)}) async-start(s32[64,1,32]{2,1,0:T(1,128)} %bitcast.2), calls=%async_computation | async-start | bytes 65536 | tf_op jit(solution)/shard_map/all_to_all | solution.py:67
  36.9 5.8 %copy-start.1 = (bf16[512,1024]{1,0:T(8,128)(2,1)S(1)}, bf16[512,1024]{1,0:T(8,128)(2,1)}, u32[]{:S(2)}) copy-start(bf16[512,1024]{1,0:T(8,128)(2,1)} %param.8) | copy-start | bytes 3145732
  55.4 196.7 %all-to-all-start.1 = ((bf16[64,64,1024]{2,1,0:T(8,128)(2,1)}), bf16[64,64,1024]{2,1,0:T(8,128)(2,1)}, u32[]{:S(2)}, u32[]{:S(2)}) async-start(bf16[64,64,1024]{2,1,0:T(8,128)(2,1)} %pad_maximum_fusion), calls=%async_computation.1 | async-start | bytes 16777216 | tf_op jit(solution)/shard_map/all_to_all | solution.py:96
  66.0 51.6 %all-reduce.4.cloned.1.call-start = ((), (), s32[]{:S(2)}) async-start(), calls=%async_computation.3 | async-start | bytes 1048576 | tf_op jit(solution)/shard_map/psum | solution.py:109
  67.9 49.7 %copy-start.8 = (s32[512]{0:T(512)S(1)}, s32[512]{0:T(512)}, u32[]{:S(2)}) copy-start(s32[512]{0:T(512)} %param.10) | copy-start | bytes 6148
  262.4 1.3 copy-start.9
  286.0 15.7 %all-to-all-start.2 = ((bf16[64,1,32]{2,1,0:T(2,128)(2,1)}), bf16[64,1,32]{2,1,0:T(2,128)(2,1)S(1)}, u32[]{:S(2)}, u32[]{:S(2)}) async-start(bf16[64,1,32]{2,1,0:T(2,128)(2,1)} %convert_element_type.101), calls=%async_computation.2 | async-start | bytes 65536 | tf_op jit(solution)/shard_map/all_to_all | solution.py:125
  292.5 4.1 %copy-start.4 = (bf16[512,512]{1,0:T(8,128)(2,1)S(1)}, bf16[512,512]{1,0:T(8,128)(2,1)}, u32[]{:S(2)}) copy-start(bf16[512,512]{1,0:T(8,128)(2,1)} %all-reduce.4.cloned.1.call-done) | copy-start | bytes 1572868
  301.8 4.7 %copy-start.2 = (f32[512,1024]{1,0:T(8,128)S(1)}, f32[512,1024]{1,0:T(8,128)}, u32[]{:S(2)}) copy-start(f32[512,1024]{1,0:T(8,128)} %bitcast_add_fusion) | copy-start | bytes 6291460
  319.1 2.4 copy-start.3
Sparse Core Ops, SparseCore 0:
  69.7 47.8 all-reduce.3
